TPU v7x, 32 devices: a whole 2x2x4 slice. The times are simulated.
32 devices in a mesh: tm: 16 (over z, y, x), atom: 2 (over core).
Axes of the slice: x: 2, y: 2, z: 4, core: 2. Of those that a mesh axis runs over, the one named last changes fastest.
Arguments:
- positions: int32 [3, 512, 512], P(None, 'tm', 'atom'), may hold values from 0 to 16383, as said below
- velocities: float32 [3, 512, 512], P(None, 'tm', 'atom'), may hold values from -6 to 6
- species: int32 [512], P('atom'), may hold values 0 or 1
- wave_vectors: int32 [3, 256], replicated, may hold values from -64 to 64
Outputs:
- isf: float32 [6, 256, 256], P(None, 'tm', 'atom')
Inputs may be any that keep to these rules, and one draw needn't show every extreme that they name: `positions`: coordinates are fixed-point fractions of the periodic box in units of 1/16384.
All inputs are finite; a program needn't handle non-finite values. No bound on the sum of `species` on one device may be relied on, other than what follows from the above.
Results may differ from a plain program's by a relative error of at most 0.0003.
Values sent between devices are 32-bit elements; how exact they have to be, the bound alone decides.
A program may use at most 64 MiB of HBM per device.

v0:
```python
import math
import jax
import jax.numpy as jnp
from jax import lax
from jax.sharding import PartitionSpec as P

WAVE_MAX = 64
highest = lax.Precision.HIGHEST


def frame_block(pos_block, vel_block, species_onehot, wave_vectors):
    summed = (
        pos_block[0][:, :, None] * wave_vectors[0]
        + pos_block[1][:, :, None] * wave_vectors[1]
        + pos_block[2][:, :, None] * wave_vectors[2]
    )
    angle_unit = jnp.float32(2.0 * math.pi / 16384.0)
    phase = jnp.remainder(summed, 16384).astype(jnp.float32) * angle_unit
    kinds = jnp.concatenate([jnp.ones_like(vel_block[:1]), vel_block], 0)
    weights = kinds[:, None] * species_onehot[None, :, None, :]
    cos_part = jnp.einsum("qsba,bak->qsbk", weights, jnp.cos(phase), precision=highest)
    sin_part = jnp.einsum("qsba,bak->qsbk", weights, jnp.sin(phase), precision=highest)
    return jnp.stack([cos_part, sin_part])


def pair_terms(cos_rows, sin_rows):
    cos_a = cos_rows[:, :, 0]
    cos_b = cos_rows[:, :, 1]
    sin_a = sin_rows[:, :, 0]
    sin_b = sin_rows[:, :, 1]
    real_part = jnp.stack(
        [
            cos_a * cos_a + sin_a * sin_a,
            cos_a * cos_b + sin_a * sin_b,
            cos_b * cos_b + sin_b * sin_b,
        ],
        2,
    ).sum(0)
    imag_part = jnp.stack(
        [
            cos_a * sin_a - sin_a * cos_a,
            cos_a * sin_b - sin_a * cos_b,
            cos_b * sin_b - sin_b * cos_b,
        ],
        2,
    ).sum(0)
    return (real_part, imag_part)


def correlate(signals, atom_total):
    frame_total = signals.shape[-1]
    waves_here = signals.shape[3]
    signal_rows = signals.reshape(-1, frame_total)
    groups = lax.axis_size("atom")
    freq_count = frame_total // groups
    lag_count = frame_total // 2 // groups
    my_index = lax.axis_index("atom")
    freq_index = my_index * freq_count + jnp.arange(freq_count, dtype=jnp.int32)
    time_index = jnp.arange(frame_total, dtype=jnp.int32)
    angle_step = jnp.float32(math.pi / frame_total)
    turns = jnp.remainder(time_index[:, None] * freq_index[None, :], 2 * frame_total)
    angles = turns.astype(jnp.float32) * angle_step
    spec_cos = jnp.dot(signal_rows, jnp.cos(angles), precision=highest).reshape(
        2, 2, 2, waves_here, freq_count
    )
    spec_sin = jnp.dot(signal_rows, jnp.sin(angles), precision=highest).reshape(
        2, 2, 2, waves_here, freq_count
    )
    real_part, imag_part = pair_terms(spec_cos, spec_sin)
    spectral_weight = jnp.where(freq_index == 0, 1.0, 2.0).astype(jnp.float32)
    real_rows = (real_part * spectral_weight).reshape(6 * waves_here, freq_count)
    imag_rows = (imag_part * spectral_weight).reshape(6 * waves_here, freq_count)
    alternating = jnp.where(time_index % 2 == 0, 1.0, -1.0).astype(jnp.float32)
    nyquist = jnp.dot(signal_rows, alternating, precision=highest).reshape(2, 2, 2, waves_here)
    nyq_a = nyquist[:, :, 0]
    nyq_b = nyquist[:, :, 1]
    nyq_real = (
        jnp.stack([nyq_a * nyq_a, nyq_a * nyq_b, nyq_b * nyq_b], 2).sum(0).reshape(6 * waves_here)
    )
    nyq_here = nyq_real * jnp.where(my_index == 0, 1.0, 0.0).astype(jnp.float32)
    lag_index = jnp.arange(lag_count * lax.axis_size("atom"), dtype=jnp.int32)
    lag_turns = jnp.remainder(lag_index[:, None] * freq_index[None, :], 2 * frame_total)
    lag_angles = lag_turns.astype(jnp.float32) * angle_step
    term = jnp.dot(jnp.cos(lag_angles), real_rows.T, precision=highest) - jnp.dot(
        jnp.sin(lag_angles), imag_rows.T, precision=highest
    )
    lag_sign = jnp.where(lag_index % 2 == 0, 1.0, -1.0).astype(jnp.float32)
    shared = lax.psum_scatter(
        term + lag_sign[:, None] * nyq_here[None, :], "atom", scatter_dimension=0, tiled=True
    )
    lag_index = my_index * lag_count + jnp.arange(lag_count, dtype=jnp.int32)
    scaled = shared / jnp.float32(2 * frame_total)
    isf = (
        scaled / (jnp.float32(atom_total) * (frame_total - lag_index).astype(jnp.float32))[:, None]
    )
    return isf.T.reshape(6, waves_here, lag_count)


def per_device(positions, velocities, species, wave_vectors):
    atom_count = positions.shape[2]
    frame_count = positions.shape[1]
    wave_count = wave_vectors.shape[1]
    block_size = math.gcd(frame_count, 2)
    block_count = frame_count // block_size
    species_onehot = jnp.stack([1 - species, species]).astype(jnp.float32)
    pos_blocks = positions.reshape(3, block_count, block_size, atom_count).transpose(1, 0, 2, 3)
    vel_blocks = velocities.reshape(3, block_count, block_size, atom_count).transpose(1, 0, 2, 3)
    raw_modes = lax.map(
        lambda operands: frame_block(operands[0], operands[1], species_onehot, wave_vectors),
        (pos_blocks, vel_blocks),
    )
    raw_modes = raw_modes.transpose(1, 2, 3, 0, 4, 5).reshape(2, 4, 2, frame_count, wave_count)
    wave_scaled = wave_vectors.astype(jnp.float32) / WAVE_MAX
    current = (
        wave_scaled[0] * raw_modes[:, 1]
        + wave_scaled[1] * raw_modes[:, 2]
        + wave_scaled[2] * raw_modes[:, 3]
    )
    modes = jnp.stack([raw_modes[:, 0], current], 1)
    atom_groups = lax.axis_size("atom")
    summed = lax.psum(modes, "atom")
    owned = lax.all_to_all(summed, "tm", split_axis=4, concat_axis=3, tiled=True)
    signals = jnp.moveaxis(owned, 3, 4)
    return correlate(signals, atom_count * atom_groups)


def solution(mesh):
    return jax.shard_map(
        per_device,
        mesh=mesh,
        in_specs=(P(None, "tm", "atom"), P(None, "tm", "atom"), P("atom"), P()),
        out_specs=P(None, "tm", "atom"),
        check_vma=False,
    )
```

profile of v0, /device:TPU:0, one launch (start us, length us, event | category | flops | bytes accessed | tf_op | source)
XLA Modules:
  0.0 160.4 jit_solution(9982431130612515028)
XLA Ops:
  9.6 81.0 %while.12 = (s32[]{:T(128)}, f32[16,2,4,2,2,256]{5,2,3,4,1,0:T(4,128)S(1)}, s32[16,3,2,256]{3,2,0,1:T(2,128)S(1)}, s32[3,256]{1,0:T(4,128)S(1)}, f32[16,3,2,256]...) while((s32[]{:T(128)}, f32[16,2,4,2,2,256]{5,2,3,4,1,0:T(4,128)S(1)}, ...), condition=%wide.region_1.2_spmd, body=%wide.region_0.1_spmd.sunk | while | flops 29900800 | bytes 194661 | solution.py:108
  12.1 2.5 %convolution_bitcast_fusion.4 = f32[1,4,2,2,256]{4,1,2,3,0:T(4,128)S(1)} fusion(s32[256]{0:T(256)S(1)} %bitcast.120, s32[2,256]{1,0:T(2,128)S(1)} %get-tuple-element.188, s32[256]{0:T(256)S(1)} %bitcast.122, s32[2,256]{1,0:T(2,128)S(1)} %get-tuple-element.190, s32[256]{0:T(256)S(1)} %bitcast.118, s32[2,256]{1,0:T(2,128)S(1)} %get-tuple-element.192, ...), kind=kOutput, calls=%fused_computation.clone.1 | convolution fusion | flops 14946304 | bytes 35840 | tf_op jit(solution)/shard_map/while/body/eval_jaxpr/qsba,bak->qsbk/dot_general | solution.py:22
  17.2 2.5 %convolution_bitcast_fusion.4 = f32[1,4,2,2,256]{4,1,2,3,0:T(4,128)S(1)} fusion(s32[256]{0:T(256)S(1)} %bitcast.120, s32[2,256]{1,0:T(2,128)S(1)} %get-tuple-element.188, s32[256]{0:T(256)S(1)} %bitcast.122, s32[2,256]{1,0:T(2,128)S(1)} %get-tuple-element.190, s32[256]{0:T(256)S(1)} %bitcast.118, s32[2,256]{1,0:T(2,128)S(1)} %get-tuple-element.192, ...), kind=kOutput, calls=%fused_computation.clone.1 | convolution fusion | flops 14946304 | bytes 35840 | tf_op jit(solution)/shard_map/while/body/eval_jaxpr/qsba,bak->qsbk/dot_general | solution.py:22
  22.2 2.5 %convolution_bitcast_fusion.4 = f32[1,4,2,2,256]{4,1,2,3,0:T(4,128)S(1)} fusion(s32[256]{0:T(256)S(1)} %bitcast.120, s32[2,256]{1,0:T(2,128)S(1)} %get-tuple-element.188, s32[256]{0:T(256)S(1)} %bitcast.122, s32[2,256]{1,0:T(2,128)S(1)} %get-tuple-element.190, s32[256]{0:T(256)S(1)} %bitcast.118, s32[2,256]{1,0:T(2,128)S(1)} %get-tuple-element.192, ...), kind=kOutput, calls=%fused_computation.clone.1 | convolution fusion | flops 14946304 | bytes 35840 | tf_op jit(solution)/shard_map/while/body/eval_jaxpr/qsba,bak->qsbk/dot_general | solution.py:22
  24.9 2.5 %convolution_bitcast_fusion.5 = f32[1,4,2,2,256]{4,1,2,3,0:T(4,128)S(1)} fusion(s32[256]{0:T(256)S(1)} %bitcast.119, s32[2,256]{1,0:T(2,128)S(1)} %get-tuple-element.188, s32[256]{0:T(256)S(1)} %bitcast.121, s32[2,256]{1,0:T(2,128)S(1)} %get-tuple-element.190, s32[256]{0:T(256)S(1)} %bitcast.117, s32[2,256]{1,0:T(2,128)S(1)} %get-tuple-element.192, ...), kind=kOutput, calls=%fused_computation.1.clone.1 | convolution fusion | flops 14946304 | bytes 35840 | tf_op jit(solution)/shard_map/while/body/eval_jaxpr/qsba,bak->qsbk/dot_general | solution.py:21
  27.3 2.5 %convolution_bitcast_fusion.4 = f32[1,4,2,2,256]{4,1,2,3,0:T(4,128)S(1)} fusion(s32[256]{0:T(256)S(1)} %bitcast.120, s32[2,256]{1,0:T(2,128)S(1)} %get-tuple-element.188, s32[256]{0:T(256)S(1)} %bitcast.122, s32[2,256]{1,0:T(2,128)S(1)} %get-tuple-element.190, s32[256]{0:T(256)S(1)} %bitcast.118, s32[2,256]{1,0:T(2,128)S(1)} %get-tuple-element.192, ...), kind=kOutput, calls=%fused_computation.clone.1 | convolution fusion | flops 14946304 | bytes 35840 | tf_op jit(solution)/shard_map/while/body/eval_jaxpr/qsba,bak->qsbk/dot_general | solution.py:22
  29.9 2.5 %convolution_bitcast_fusion.5 = f32[1,4,2,2,256]{4,1,2,3,0:T(4,128)S(1)} fusion(s32[256]{0:T(256)S(1)} %bitcast.119, s32[2,256]{1,0:T(2,128)S(1)} %get-tuple-element.188, s32[256]{0:T(256)S(1)} %bitcast.121, s32[2,256]{1,0:T(2,128)S(1)} %get-tuple-element.190, s32[256]{0:T(256)S(1)} %bitcast.117, s32[2,256]{1,0:T(2,128)S(1)} %get-tuple-element.192, ...), kind=kOutput, calls=%fused_computation.1.clone.1 | convolution fusion | flops 14946304 | bytes 35840 | tf_op jit(solution)/shard_map/while/body/eval_jaxpr/qsba,bak->qsbk/dot_general | solution.py:21
  32.4 2.5 %convolution_bitcast_fusion.4 = f32[1,4,2,2,256]{4,1,2,3,0:T(4,128)S(1)} fusion(s32[256]{0:T(256)S(1)} %bitcast.120, s32[2,256]{1,0:T(2,128)S(1)} %get-tuple-element.188, s32[256]{0:T(256)S(1)} %bitcast.122, s32[2,256]{1,0:T(2,128)S(1)} %get-tuple-element.190, s32[256]{0:T(256)S(1)} %bitcast.118, s32[2,256]{1,0:T(2,128)S(1)} %get-tuple-element.192, ...), kind=kOutput, calls=%fused_computation.clone.1 | convolution fusion | flops 14946304 | bytes 35840 | tf_op jit(solution)/shard_map/while/body/eval_jaxpr/qsba,bak->qsbk/dot_general | solution.py:22
  37.4 2.5 %convolution_bitcast_fusion.4 = f32[1,4,2,2,256]{4,1,2,3,0:T(4,128)S(1)} fusion(s32[256]{0:T(256)S(1)} %bitcast.120, s32[2,256]{1,0:T(2,128)S(1)} %get-tuple-element.188, s32[256]{0:T(256)S(1)} %bitcast.122, s32[2,256]{1,0:T(2,128)S(1)} %get-tuple-element.190, s32[256]{0:T(256)S(1)} %bitcast.118, s32[2,256]{1,0:T(2,128)S(1)} %get-tuple-element.192, ...), kind=kOutput, calls=%fused_computation.clone.1 | convolution fusion | flops 14946304 | bytes 35840 | tf_op jit(solution)/shard_map/while/body/eval_jaxpr/qsba,bak->qsbk/dot_general | solution.py:22
  42.5 2.5 %convolution_bitcast_fusion.4 = f32[1,4,2,2,256]{4,1,2,3,0:T(4,128)S(1)} fusion(s32[256]{0:T(256)S(1)} %bitcast.120, s32[2,256]{1,0:T(2,128)S(1)} %get-tuple-element.188, s32[256]{0:T(256)S(1)} %bitcast.122, s32[2,256]{1,0:T(2,128)S(1)} %get-tuple-element.190, s32[256]{0:T(256)S(1)} %bitcast.118, s32[2,256]{1,0:T(2,128)S(1)} %get-tuple-element.192, ...), kind=kOutput, calls=%fused_computation.clone.1 | convolution fusion | flops 14946304 | bytes 35840 | tf_op jit(solution)/shard_map/while/body/eval_jaxpr/qsba,bak->qsbk/dot_general | solution.py:22
  47.6 2.5 %convolution_bitcast_fusion.4 = f32[1,4,2,2,256]{4,1,2,3,0:T(4,128)S(1)} fusion(s32[256]{0:T(256)S(1)} %bitcast.120, s32[2,256]{1,0:T(2,128)S(1)} %get-tuple-element.188, s32[256]{0:T(256)S(1)} %bitcast.122, s32[2,256]{1,0:T(2,128)S(1)} %get-tuple-element.190, s32[256]{0:T(256)S(1)} %bitcast.118, s32[2,256]{1,0:T(2,128)S(1)} %get-tuple-element.192, ...), kind=kOutput, calls=%fused_computation.clone.1 | convolution fusion | flops 14946304 | bytes 35840 | tf_op jit(solution)/shard_map/while/body/eval_jaxpr/qsba,bak->qsbk/dot_general | solution.py:22
  50.2 2.5 %convolution_bitcast_fusion.5 = f32[1,4,2,2,256]{4,1,2,3,0:T(4,128)S(1)} fusion(s32[256]{0:T(256)S(1)} %bitcast.119, s32[2,256]{1,0:T(2,128)S(1)} %get-tuple-element.188, s32[256]{0:T(256)S(1)} %bitcast.121, s32[2,256]{1,0:T(2,128)S(1)} %get-tuple-element.190, s32[256]{0:T(256)S(1)} %bitcast.117, s32[2,256]{1,0:T(2,128)S(1)} %get-tuple-element.192, ...), kind=kOutput, calls=%fused_computation.1.clone.1 | convolution fusion | flops 14946304 | bytes 35840 | tf_op jit(solution)/shard_map/while/body/eval_jaxpr/qsba,bak->qsbk/dot_general | solution.py:21
  52.6 2.5 %convolution_bitcast_fusion.4 = f32[1,4,2,2,256]{4,1,2,3,0:T(4,128)S(1)} fusion(s32[256]{0:T(256)S(1)} %bitcast.120, s32[2,256]{1,0:T(2,128)S(1)} %get-tuple-element.188, s32[256]{0:T(256)S(1)} %bitcast.122, s32[2,256]{1,0:T(2,128)S(1)} %get-tuple-element.190, s32[256]{0:T(256)S(1)} %bitcast.118, s32[2,256]{1,0:T(2,128)S(1)} %get-tuple-element.192, ...), kind=kOutput, calls=%fused_computation.clone.1 | convolution fusion | flops 14946304 | bytes 35840 | tf_op jit(solution)/shard_map/while/body/eval_jaxpr/qsba,bak->qsbk/dot_general | solution.py:22
  57.7 2.5 %convolution_bitcast_fusion.4 = f32[1,4,2,2,256]{4,1,2,3,0:T(4,128)S(1)} fusion(s32[256]{0:T(256)S(1)} %bitcast.120, s32[2,256]{1,0:T(2,128)S(1)} %get-tuple-element.188, s32[256]{0:T(256)S(1)} %bitcast.122, s32[2,256]{1,0:T(2,128)S(1)} %get-tuple-element.190, s32[256]{0:T(256)S(1)} %bitcast.118, s32[2,256]{1,0:T(2,128)S(1)} %get-tuple-element.192, ...), kind=kOutput, calls=%fused_computation.clone.1 | convolution fusion | flops 14946304 | bytes 35840 | tf_op jit(solution)/shard_map/while/body/eval_jaxpr/qsba,bak->qsbk/dot_general | solution.py:22
  62.8 2.5 %convolution_bitcast_fusion.4 = f32[1,4,2,2,256]{4,1,2,3,0:T(4,128)S(1)} fusion(s32[256]{0:T(256)S(1)} %bitcast.120, s32[2,256]{1,0:T(2,128)S(1)} %get-tuple-element.188, s32[256]{0:T(256)S(1)} %bitcast.122, s32[2,256]{1,0:T(2,128)S(1)} %get-tuple-element.190, s32[256]{0:T(256)S(1)} %bitcast.118, s32[2,256]{1,0:T(2,128)S(1)} %get-tuple-element.192, ...), kind=kOutput, calls=%fused_computation.clone.1 | convolution fusion | flops 14946304 | bytes 35840 | tf_op jit(solution)/shard_map/while/body/eval_jaxpr/qsba,bak->qsbk/dot_general | solution.py:22
  67.8 2.5 %convolution_bitcast_fusion.4 = f32[1,4,2,2,256]{4,1,2,3,0:T(4,128)S(1)} fusion(s32[256]{0:T(256)S(1)} %bitcast.120, s32[2,256]{1,0:T(2,128)S(1)} %get-tuple-element.188, s32[256]{0:T(256)S(1)} %bitcast.122, s32[2,256]{1,0:T(2,128)S(1)} %get-tuple-element.190, s32[256]{0:T(256)S(1)} %bitcast.118, s32[2,256]{1,0:T(2,128)S(1)} %get-tuple-element.192, ...), kind=kOutput, calls=%fused_computation.clone.1 | convolution fusion | flops 14946304 | bytes 35840 | tf_op jit(solution)/shard_map/while/body/eval_jaxpr/qsba,bak->qsbk/dot_general | solution.py:22
  72.9 2.5 %convolution_bitcast_fusion.4 = f32[1,4,2,2,256]{4,1,2,3,0:T(4,128)S(1)} fusion(s32[256]{0:T(256)S(1)} %bitcast.120, s32[2,256]{1,0:T(2,128)S(1)} %get-tuple-element.188, s32[256]{0:T(256)S(1)} %bitcast.122, s32[2,256]{1,0:T(2,128)S(1)} %get-tuple-element.190, s32[256]{0:T(256)S(1)} %bitcast.118, s32[2,256]{1,0:T(2,128)S(1)} %get-tuple-element.192, ...), kind=kOutput, calls=%fused_computation.clone.1 | convolution fusion | flops 14946304 | bytes 35840 | tf_op jit(solution)/shard_map/while/body/eval_jaxpr/qsba,bak->qsbk/dot_general | solution.py:22
  78.0 2.5 %convolution_bitcast_fusion.4 = f32[1,4,2,2,256]{4,1,2,3,0:T(4,128)S(1)} fusion(s32[256]{0:T(256)S(1)} %bitcast.120, s32[2,256]{1,0:T(2,128)S(1)} %get-tuple-element.188, s32[256]{0:T(256)S(1)} %bitcast.122, s32[2,256]{1,0:T(2,128)S(1)} %get-tuple-element.190, s32[256]{0:T(256)S(1)} %bitcast.118, s32[2,256]{1,0:T(2,128)S(1)} %get-tuple-element.192, ...), kind=kOutput, calls=%fused_computation.clone.1 | convolution fusion | flops 14946304 | bytes 35840 | tf_op jit(solution)/shard_map/while/body/eval_jaxpr/qsba,bak->qsbk/dot_general | solution.py:22
  83.0 2.5 %convolution_bitcast_fusion.4 = f32[1,4,2,2,256]{4,1,2,3,0:T(4,128)S(1)} fusion(s32[256]{0:T(256)S(1)} %bitcast.120, s32[2,256]{1,0:T(2,128)S(1)} %get-tuple-element.188, s32[256]{0:T(256)S(1)} %bitcast.122, s32[2,256]{1,0:T(2,128)S(1)} %get-tuple-element.190, s32[256]{0:T(256)S(1)} %bitcast.118, s32[2,256]{1,0:T(2,128)S(1)} %get-tuple-element.192, ...), kind=kOutput, calls=%fused_computation.clone.1 | convolution fusion | flops 14946304 | bytes 35840 | tf_op jit(solution)/shard_map/while/body/eval_jaxpr/qsba,bak->qsbk/dot_general | solution.py:22
  88.1 2.5 %convolution_bitcast_fusion.4 = f32[1,4,2,2,256]{4,1,2,3,0:T(4,128)S(1)} fusion(s32[256]{0:T(256)S(1)} %bitcast.120, s32[2,256]{1,0:T(2,128)S(1)} %get-tuple-element.188, s32[256]{0:T(256)S(1)} %bitcast.122, s32[2,256]{1,0:T(2,128)S(1)} %get-tuple-element.190, s32[256]{0:T(256)S(1)} %bitcast.118, s32[2,256]{1,0:T(2,128)S(1)} %get-tuple-element.192, ...), kind=kOutput, calls=%fused_computation.clone.1 | convolution fusion | flops 14946304 | bytes 35840 | tf_op jit(solution)/shard_map/while/body/eval_jaxpr/qsba,bak->qsbk/dot_general | solution.py:22
  91.9 21.1 %all-reduce.3.cloned.1.call-done = f32[2,2,2,32,256]{4,2,3,1,0:T(2,128)} async-done(((f32[2,2,2,32,256]{4,2,3,1,0:T(2,128)}), f32[2,2,2,32,256]{4,2,3,1,0:T(2,128)}) %all-reduce.3.cloned.1.call-update) | async-done | bytes 262160 | tf_op jit(solution)/shard_map/psum | solution.py:121
  116.4 6.8 %all-to-all-start = ((f32[16,1,4096]{2,1,0:T(1,128)}), f32[16,1,4096]{2,1,0:T(1,128)S(1)}, u32[]{:S(2)}, u32[]{:S(2)}) async-start(f32[16,1,4096]{2,1,0:T(1,128)} %reshape.89), calls=%async_computation | async-start | bytes 524288 | tf_op jit(solution)/shard_map/all_to_all | solution.py:122
  123.5 10.0 %all-to-all-done = f32[16,1,4096]{2,1,0:T(1,128)S(1)} async-done(((f32[16,1,4096]{2,1,0:T(1,128)}), f32[16,1,4096]{2,1,0:T(1,128)S(1)}, u32[]{:S(2)}, u32[]{:S(2)}) %all-to-all-start) | async-done | bytes 262176 | tf_op jit(solution)/shard_map/all_to_all | solution.py:122
  146.5 5.6 %reduce-scatter.2.cloned.1.call-done = f32[128,96]{0,1:T(8,128)} async-done(((f32[256,96]{0,1:T(8,128)}), f32[128,96]{0,1:T(8,128)}) %reduce-scatter.2.cloned.1.call-update) | async-done | bytes 49168 | tf_op jit(solution)/shard_map/reduce_scatter | solution.py:88
  (157 shorter events, 55.1 us)
Async XLA Ops:
  6.5 106.5 %all-reduce.3.cloned.1.call-start = ((), (), s32[]{:S(2)}) async-start(), calls=%async_computation.2 | async-start | bytes 524288 | tf_op jit(solution)/shard_map/psum | solution.py:121
  7.2 1.0 copy-start
  8.2 0.7 copy-start.2
  8.9 0.7 copy-start.1
  116.4 17.1 %all-to-all-start = ((f32[16,1,4096]{2,1,0:T(1,128)}), f32[16,1,4096]{2,1,0:T(1,128)S(1)}, u32[]{:S(2)}, u32[]{:S(2)}) async-start(f32[16,1,4096]{2,1,0:T(1,128)} %reshape.89), calls=%async_computation | async-start | bytes 524288 | tf_op jit(solution)/shard_map/all_to_all | solution.py:122
  123.2 28.9 %reduce-scatter.2.cloned.1.call-start = ((), (), s32[]{:S(2)}) async-start(), calls=%async_computation.3 | async-start | bytes 147456 | tf_op jit(solution)/shard_map/reduce_scatter | solution.py:88
Sparse Core Ops, SparseCore 0:
  92.0 20.9 all-reduce.2
  146.7 5.4 reduce-scatter.1
where the time goes:
time: 161 us; the launch traced here: 160 us
  matrix products  88.1 us (55%)
  waiting for transfers between devices  36.8 us (23%)
  between operations  13.6 us (8%)
  local copies, waits for them, and re-layouts  8.99 us (6%)
  starting transfers between devices  7.01 us (4%)
  other arithmetic  4.92 us (3%)
    dot_general x16, matrix products, frame_block(): jnp.einsum('qsba,bak->qsbk', weights, jnp.sin(phase), precision=highest)  39.8 us
    dot_general x16, matrix products, frame_block(): jnp.einsum('qsba,bak->qsbk', weights, jnp.cos(phase), precision=highest)  39.3 us
    psum x1, waiting for transfers between devices, per_device(): summed = lax.psum(modes, 'atom')  21.1 us
    all_to_all x1, waiting for transfers between devices, per_device(): lax.all_to_all(summed, 'tm', split_axis=4, concat_axis=3, tiled=True)  10 us
    all_to_all x1, starting transfers between devices, per_device(): lax.all_to_all(summed, 'tm', split_axis=4, concat_axis=3, tiled=True)  6.78 us
    reduce_scatter x1, waiting for transfers between devices, correlate(): lax.psum_scatter(term + lag_sign[:, None] * nyq_here[None, :], 'atom', sc...  5.55 us
    unnamed x9, local copies, waits for them, and re-layouts  4.93 us
  transfers between devices with their start and end apart: 3, of which 3 were waited for; matrix products, arithmetic and copies ran while one was open for 0% of the time, Pallas kernels for 0%

commit v1 on v0

--- a/solution.py
+++ b/solution.py
@@ -119,7 +119,10 @@
     modes = jnp.stack([raw_modes[:, 0], current], 1)
     atom_groups = lax.axis_size("atom")
     summed = lax.psum(modes, "atom")
-    owned = lax.all_to_all(summed, "tm", split_axis=4, concat_axis=3, tiled=True)
+    owned = jnp.concatenate(
+        lax.all_to_all(jnp.stack(jnp.split(summed, lax.axis_size("tm"), axis=4)), "tm", 0, 0),
+        axis=3,
+    )
     signals = jnp.moveaxis(owned, 3, 4)
     return correlate(signals, atom_count * atom_groups)
 

time: 161 us -> 184 us (1.14)
  local copies, waits for them, and re-layouts: 8.99 us -> 30.6 us
    slice x16, local copies, waits for them, and re-layouts: 0.08 us -> 12.9 us  [frame_block(): wave_vectors[0]]
    unnamed x9 -> x20, local copies, waits for them, and re-layouts: 4.93 us -> 13.1 us
where the time goes in v1:
time: 184 us; the launch traced here: 183 us
  matrix products  88.1 us (48%)
  waiting for transfers between devices  36.7 us (20%)
  local copies, waits for them, and re-layouts  30.6 us (17%)
  between operations  13.7 us (7%)
  starting transfers between devices  7.01 us (4%)
  other arithmetic  6.27 us (3%)
    dot_general x16, matrix products, frame_block(): jnp.einsum('qsba,bak->qsbk', weights, jnp.sin(phase), precision=highest)  39.8 us
    dot_general x16, matrix products, frame_block(): jnp.einsum('qsba,bak->qsbk', weights, jnp.cos(phase), precision=highest)  39.3 us
    psum x1, waiting for transfers between devices, per_device(): summed = lax.psum(modes, 'atom')  21.1 us
    unnamed x20, local copies, waits for them, and re-layouts  13.1 us
    slice x16, local copies, waits for them, and re-layouts, frame_block(): wave_vectors[0]  12.9 us
    all_to_all x1, waiting for transfers between devices, per_device(): lax.all_to_all(jnp.stack(jnp.split(summed, lax.axis_size('tm'), axis=4)),...  10 us
    all_to_all x1, starting transfers between devices, per_device(): lax.all_to_all(jnp.stack(jnp.split(summed, lax.axis_size('tm'), axis=4)),...  6.78 us
    reduce_scatter x1, waiting for transfers between devices, correlate(): lax.psum_scatter(term + lag_sign[:, None] * nyq_here[None, :], 'atom', sc...  5.53 us
  transfers between devices with their start and end apart: 3, of which 3 were waited for; matrix products, arithmetic and copies ran while one was open for 0% of the time, Pallas kernels for 0%

profile of v1, /device:TPU:0, one launch (start us, length us, event | category | flops | bytes accessed | tf_op | source)
XLA Modules:
  0.0 183.2 jit_solution(5930904032424987819)
XLA Ops:
  10.5 93.6 %while.12 = (s32[]{:T(128)}, f32[16,2,4,2,2,256]{5,2,3,4,1,0:T(4,128)S(1)}, s32[16,3,2,256]{3,2,0,1:T(2,128)S(1)}, s32[3,256]{1,0:T(4,128)}, f32[16,3,2,256]{3,1...) while((s32[]{:T(128)}, f32[16,2,4,2,2,256]{5,2,3,4,1,0:T(4,128)S(1)}, ...), condition=%wide.region_1.2_spmd, body=%wide.region_0.1_spmd.sunk | while | flops 29900800 | bytes 194661 | solution.py:108
  11.4 2.5 %convolution_bitcast_fusion.5 = f32[1,4,2,2,256]{4,1,2,3,0:T(4,128)S(1)} fusion(s32[256]{0:T(256)S(1)} %bitcast.181, s32[2,256]{1,0:T(2,128)S(1)} %get-tuple-element.182, s32[256]{0:T(256)S(1)} %bitcast.183, s32[2,256]{1,0:T(2,128)S(1)} %get-tuple-element.184, s32[256]{0:T(256)S(1)} %bitcast.179, s32[2,256]{1,0:T(2,128)S(1)} %get-tuple-element.186, ...), kind=kOutput, calls=%fused_computation.1.clone.1 | convolution fusion | flops 14946304 | bytes 35840 | tf_op jit(solution)/shard_map/while/body/eval_jaxpr/qsba,bak->qsbk/dot_general | solution.py:21
  13.8 2.5 %convolution_bitcast_fusion.4 = f32[1,4,2,2,256]{4,1,2,3,0:T(4,128)S(1)} fusion(s32[256]{0:T(256)S(1)} %bitcast.182, s32[2,256]{1,0:T(2,128)S(1)} %get-tuple-element.182, s32[256]{0:T(256)S(1)} %bitcast.184, s32[2,256]{1,0:T(2,128)S(1)} %get-tuple-element.184, s32[256]{0:T(256)S(1)} %bitcast.180, s32[2,256]{1,0:T(2,128)S(1)} %get-tuple-element.186, ...), kind=kOutput, calls=%fused_computation.clone.1 | convolution fusion | flops 14946304 | bytes 35840 | tf_op jit(solution)/shard_map/while/body/eval_jaxpr/qsba,bak->qsbk/dot_general | solution.py:22
  17.2 2.5 %convolution_bitcast_fusion.5 = f32[1,4,2,2,256]{4,1,2,3,0:T(4,128)S(1)} fusion(s32[256]{0:T(256)S(1)} %bitcast.181, s32[2,256]{1,0:T(2,128)S(1)} %get-tuple-element.182, s32[256]{0:T(256)S(1)} %bitcast.183, s32[2,256]{1,0:T(2,128)S(1)} %get-tuple-element.184, s32[256]{0:T(256)S(1)} %bitcast.179, s32[2,256]{1,0:T(2,128)S(1)} %get-tuple-element.186, ...), kind=kOutput, calls=%fused_computation.1.clone.1 | convolution fusion | flops 14946304 | bytes 35840 | tf_op jit(solution)/shard_map/while/body/eval_jaxpr/qsba,bak->qsbk/dot_general | solution.py:21
  19.7 2.5 %convolution_bitcast_fusion.4 = f32[1,4,2,2,256]{4,1,2,3,0:T(4,128)S(1)} fusion(s32[256]{0:T(256)S(1)} %bitcast.182, s32[2,256]{1,0:T(2,128)S(1)} %get-tuple-element.182, s32[256]{0:T(256)S(1)} %bitcast.184, s32[2,256]{1,0:T(2,128)S(1)} %get-tuple-element.184, s32[256]{0:T(256)S(1)} %bitcast.180, s32[2,256]{1,0:T(2,128)S(1)} %get-tuple-element.186, ...), kind=kOutput, calls=%fused_computation.clone.1 | convolution fusion | flops 14946304 | bytes 35840 | tf_op jit(solution)/shard_map/while/body/eval_jaxpr/qsba,bak->qsbk/dot_general | solution.py:22
  23.1 2.5 %convolution_bitcast_fusion.5 = f32[1,4,2,2,256]{4,1,2,3,0:T(4,128)S(1)} fusion(s32[256]{0:T(256)S(1)} %bitcast.181, s32[2,256]{1,0:T(2,128)S(1)} %get-tuple-element.182, s32[256]{0:T(256)S(1)} %bitcast.183, s32[2,256]{1,0:T(2,128)S(1)} %get-tuple-element.184, s32[256]{0:T(256)S(1)} %bitcast.179, s32[2,256]{1,0:T(2,128)S(1)} %get-tuple-element.186, ...), kind=kOutput, calls=%fused_computation.1.clone.1 | convolution fusion | flops 14946304 | bytes 35840 | tf_op jit(solution)/shard_map/while/body/eval_jaxpr/qsba,bak->qsbk/dot_general | solution.py:21
  25.5 2.5 %convolution_bitcast_fusion.4 = f32[1,4,2,2,256]{4,1,2,3,0:T(4,128)S(1)} fusion(s32[256]{0:T(256)S(1)} %bitcast.182, s32[2,256]{1,0:T(2,128)S(1)} %get-tuple-element.182, s32[256]{0:T(256)S(1)} %bitcast.184, s32[2,256]{1,0:T(2,128)S(1)} %get-tuple-element.184, s32[256]{0:T(256)S(1)} %bitcast.180, s32[2,256]{1,0:T(2,128)S(1)} %get-tuple-element.186, ...), kind=kOutput, calls=%fused_computation.clone.1 | convolution fusion | flops 14946304 | bytes 35840 | tf_op jit(solution)/shard_map/while/body/eval_jaxpr/qsba,bak->qsbk/dot_general | solution.py:22
  31.4 2.5 %convolution_bitcast_fusion.4 = f32[1,4,2,2,256]{4,1,2,3,0:T(4,128)S(1)} fusion(s32[256]{0:T(256)S(1)} %bitcast.182, s32[2,256]{1,0:T(2,128)S(1)} %get-tuple-element.182, s32[256]{0:T(256)S(1)} %bitcast.184, s32[2,256]{1,0:T(2,128)S(1)} %get-tuple-element.184, s32[256]{0:T(256)S(1)} %bitcast.180, s32[2,256]{1,0:T(2,128)S(1)} %get-tuple-element.186, ...), kind=kOutput, calls=%fused_computation.clone.1 | convolution fusion | flops 14946304 | bytes 35840 | tf_op jit(solution)/shard_map/while/body/eval_jaxpr/qsba,bak->qsbk/dot_general | solution.py:22
  37.2 2.5 %convolution_bitcast_fusion.4 = f32[1,4,2,2,256]{4,1,2,3,0:T(4,128)S(1)} fusion(s32[256]{0:T(256)S(1)} %bitcast.182, s32[2,256]{1,0:T(2,128)S(1)} %get-tuple-element.182, s32[256]{0:T(256)S(1)} %bitcast.184, s32[2,256]{1,0:T(2,128)S(1)} %get-tuple-element.184, s32[256]{0:T(256)S(1)} %bitcast.180, s32[2,256]{1,0:T(2,128)S(1)} %get-tuple-element.186, ...), kind=kOutput, calls=%fused_computation.clone.1 | convolution fusion | flops 14946304 | bytes 35840 | tf_op jit(solution)/shard_map/while/body/eval_jaxpr/qsba,bak->qsbk/dot_general | solution.py:22
  43.1 2.5 %convolution_bitcast_fusion.4 = f32[1,4,2,2,256]{4,1,2,3,0:T(4,128)S(1)} fusion(s32[256]{0:T(256)S(1)} %bitcast.182, s32[2,256]{1,0:T(2,128)S(1)} %get-tuple-element.182, s32[256]{0:T(256)S(1)} %bitcast.184, s32[2,256]{1,0:T(2,128)S(1)} %get-tuple-element.184, s32[256]{0:T(256)S(1)} %bitcast.180, s32[2,256]{1,0:T(2,128)S(1)} %get-tuple-element.186, ...), kind=kOutput, calls=%fused_computation.clone.1 | convolution fusion | flops 14946304 | bytes 35840 | tf_op jit(solution)/shard_map/while/body/eval_jaxpr/qsba,bak->qsbk/dot_general | solution.py:22
  49.0 2.5 %convolution_bitcast_fusion.4 = f32[1,4,2,2,256]{4,1,2,3,0:T(4,128)S(1)} fusion(s32[256]{0:T(256)S(1)} %bitcast.182, s32[2,256]{1,0:T(2,128)S(1)} %get-tuple-element.182, s32[256]{0:T(256)S(1)} %bitcast.184, s32[2,256]{1,0:T(2,128)S(1)} %get-tuple-element.184, s32[256]{0:T(256)S(1)} %bitcast.180, s32[2,256]{1,0:T(2,128)S(1)} %get-tuple-element.186, ...), kind=kOutput, calls=%fused_computation.clone.1 | convolution fusion | flops 14946304 | bytes 35840 | tf_op jit(solution)/shard_map/while/body/eval_jaxpr/qsba,bak->qsbk/dot_general | solution.py:22
  54.8 2.5 %convolution_bitcast_fusion.4 = f32[1,4,2,2,256]{4,1,2,3,0:T(4,128)S(1)} fusion(s32[256]{0:T(256)S(1)} %bitcast.182, s32[2,256]{1,0:T(2,128)S(1)} %get-tuple-element.182, s32[256]{0:T(256)S(1)} %bitcast.184, s32[2,256]{1,0:T(2,128)S(1)} %get-tuple-element.184, s32[256]{0:T(256)S(1)} %bitcast.180, s32[2,256]{1,0:T(2,128)S(1)} %get-tuple-element.186, ...), kind=kOutput, calls=%fused_computation.clone.1 | convolution fusion | flops 14946304 | bytes 35840 | tf_op jit(solution)/shard_map/while/body/eval_jaxpr/qsba,bak->qsbk/dot_general | solution.py:22
  60.7 2.5 %convolution_bitcast_fusion.4 = f32[1,4,2,2,256]{4,1,2,3,0:T(4,128)S(1)} fusion(s32[256]{0:T(256)S(1)} %bitcast.182, s32[2,256]{1,0:T(2,128)S(1)} %get-tuple-element.182, s32[256]{0:T(256)S(1)} %bitcast.184, s32[2,256]{1,0:T(2,128)S(1)} %get-tuple-element.184, s32[256]{0:T(256)S(1)} %bitcast.180, s32[2,256]{1,0:T(2,128)S(1)} %get-tuple-element.186, ...), kind=kOutput, calls=%fused_computation.clone.1 | convolution fusion | flops 14946304 | bytes 35840 | tf_op jit(solution)/shard_map/while/body/eval_jaxpr/qsba,bak->qsbk/dot_general | solution.py:22
  66.5 2.5 %convolution_bitcast_fusion.4 = f32[1,4,2,2,256]{4,1,2,3,0:T(4,128)S(1)} fusion(s32[256]{0:T(256)S(1)} %bitcast.182, s32[2,256]{1,0:T(2,128)S(1)} %get-tuple-element.182, s32[256]{0:T(256)S(1)} %bitcast.184, s32[2,256]{1,0:T(2,128)S(1)} %get-tuple-element.184, s32[256]{0:T(256)S(1)} %bitcast.180, s32[2,256]{1,0:T(2,128)S(1)} %get-tuple-element.186, ...), kind=kOutput, calls=%fused_computation.clone.1 | convolution fusion | flops 14946304 | bytes 35840 | tf_op jit(solution)/shard_map/while/body/eval_jaxpr/qsba,bak->qsbk/dot_general | solution.py:22
  72.4 2.5 %convolution_bitcast_fusion.4 = f32[1,4,2,2,256]{4,1,2,3,0:T(4,128)S(1)} fusion(s32[256]{0:T(256)S(1)} %bitcast.182, s32[2,256]{1,0:T(2,128)S(1)} %get-tuple-element.182, s32[256]{0:T(256)S(1)} %bitcast.184, s32[2,256]{1,0:T(2,128)S(1)} %get-tuple-element.184, s32[256]{0:T(256)S(1)} %bitcast.180, s32[2,256]{1,0:T(2,128)S(1)} %get-tuple-element.186, ...), kind=kOutput, calls=%fused_computation.clone.1 | convolution fusion | flops 14946304 | bytes 35840 | tf_op jit(solution)/shard_map/while/body/eval_jaxpr/qsba,bak->qsbk/dot_general | solution.py:22
  78.2 2.5 %convolution_bitcast_fusion.4 = f32[1,4,2,2,256]{4,1,2,3,0:T(4,128)S(1)} fusion(s32[256]{0:T(256)S(1)} %bitcast.182, s32[2,256]{1,0:T(2,128)S(1)} %get-tuple-element.182, s32[256]{0:T(256)S(1)} %bitcast.184, s32[2,256]{1,0:T(2,128)S(1)} %get-tuple-element.184, s32[256]{0:T(256)S(1)} %bitcast.180, s32[2,256]{1,0:T(2,128)S(1)} %get-tuple-element.186, ...), kind=kOutput, calls=%fused_computation.clone.1 | convolution fusion | flops 14946304 | bytes 35840 | tf_op jit(solution)/shard_map/while/body/eval_jaxpr/qsba,bak->qsbk/dot_general | solution.py:22
  84.1 2.5 %convolution_bitcast_fusion.4 = f32[1,4,2,2,256]{4,1,2,3,0:T(4,128)S(1)} fusion(s32[256]{0:T(256)S(1)} %bitcast.182, s32[2,256]{1,0:T(2,128)S(1)} %get-tuple-element.182, s32[256]{0:T(256)S(1)} %bitcast.184, s32[2,256]{1,0:T(2,128)S(1)} %get-tuple-element.184, s32[256]{0:T(256)S(1)} %bitcast.180, s32[2,256]{1,0:T(2,128)S(1)} %get-tuple-element.186, ...), kind=kOutput, calls=%fused_computation.clone.1 | convolution fusion | flops 14946304 | bytes 35840 | tf_op jit(solution)/shard_map/while/body/eval_jaxpr/qsba,bak->qsbk/dot_general | solution.py:22
  89.9 2.5 %convolution_bitcast_fusion.4 = f32[1,4,2,2,256]{4,1,2,3,0:T(4,128)S(1)} fusion(s32[256]{0:T(256)S(1)} %bitcast.182, s32[2,256]{1,0:T(2,128)S(1)} %get-tuple-element.182, s32[256]{0:T(256)S(1)} %bitcast.184, s32[2,256]{1,0:T(2,128)S(1)} %get-tuple-element.184, s32[256]{0:T(256)S(1)} %bitcast.180, s32[2,256]{1,0:T(2,128)S(1)} %get-tuple-element.186, ...), kind=kOutput, calls=%fused_computation.clone.1 | convolution fusion | flops 14946304 | bytes 35840 | tf_op jit(solution)/shard_map/while/body/eval_jaxpr/qsba,bak->qsbk/dot_general | solution.py:22
  95.8 2.5 %convolution_bitcast_fusion.4 = f32[1,4,2,2,256]{4,1,2,3,0:T(4,128)S(1)} fusion(s32[256]{0:T(256)S(1)} %bitcast.182, s32[2,256]{1,0:T(2,128)S(1)} %get-tuple-element.182, s32[256]{0:T(256)S(1)} %bitcast.184, s32[2,256]{1,0:T(2,128)S(1)} %get-tuple-element.184, s32[256]{0:T(256)S(1)} %bitcast.180, s32[2,256]{1,0:T(2,128)S(1)} %get-tuple-element.186, ...), kind=kOutput, calls=%fused_computation.clone.1 | convolution fusion | flops 14946304 | bytes 35840 | tf_op jit(solution)/shard_map/while/body/eval_jaxpr/qsba,bak->qsbk/dot_general | solution.py:22
  101.7 2.5 %convolution_bitcast_fusion.4 = f32[1,4,2,2,256]{4,1,2,3,0:T(4,128)S(1)} fusion(s32[256]{0:T(256)S(1)} %bitcast.182, s32[2,256]{1,0:T(2,128)S(1)} %get-tuple-element.182, s32[256]{0:T(256)S(1)} %bitcast.184, s32[2,256]{1,0:T(2,128)S(1)} %get-tuple-element.184, s32[256]{0:T(256)S(1)} %bitcast.180, s32[2,256]{1,0:T(2,128)S(1)} %get-tuple-element.186, ...), kind=kOutput, calls=%fused_computation.clone.1 | convolution fusion | flops 14946304 | bytes 35840 | tf_op jit(solution)/shard_map/while/body/eval_jaxpr/qsba,bak->qsbk/dot_general | solution.py:22
  105.4 21.1 %all-reduce.3.cloned.1.call-done = f32[2,2,2,32,256]{4,2,3,1,0:T(2,128)} async-done(((f32[2,2,2,32,256]{4,2,3,1,0:T(2,128)}), f32[2,2,2,32,256]{4,2,3,1,0:T(2,128)}) %all-reduce.3.cloned.1.call-update) | async-done | bytes 262160 | tf_op jit(solution)/shard_map/psum | solution.py:121
  139.7 6.8 %all-to-all-start = ((f32[16,1,4096]{2,1,0:T(1,128)}), f32[16,1,4096]{2,1,0:T(1,128)S(1)}, u32[]{:S(2)}, u32[]{:S(2)}) async-start(f32[16,1,4096]{2,1,0:T(1,128)} %reshape.97), calls=%async_computation | async-start | bytes 524288 | tf_op jit(solution)/shard_map/all_to_all | solution.py:123
  146.8 10.0 %all-to-all-done = f32[16,1,4096]{2,1,0:T(1,128)S(1)} async-done(((f32[16,1,4096]{2,1,0:T(1,128)}), f32[16,1,4096]{2,1,0:T(1,128)S(1)}, u32[]{:S(2)}, u32[]{:S(2)}) %all-to-all-start) | async-done | bytes 262176 | tf_op jit(solution)/shard_map/all_to_all | solution.py:123
  169.5 5.5 %reduce-scatter.2.cloned.1.call-done = f32[128,96]{0,1:T(8,128)} async-done(((f32[256,96]{0,1:T(8,128)}), f32[128,96]{0,1:T(8,128)}) %reduce-scatter.2.cloned.1.call-update) | async-done | bytes 49168 | tf_op jit(solution)/shard_map/reduce_scatter | solution.py:88
  (169 shorter events, 78.1 us)
Async XLA Ops:
  6.5 120.0 %all-reduce.3.cloned.1.call-start = ((), (), s32[]{:S(2)}) async-start(), calls=%async_computation.2 | async-start | bytes 524288 | tf_op jit(solution)/shard_map/psum | solution.py:121
  126.6 9.1 %copy-start = (f32[2,2,2,32,256]{4,2,3,1,0:T(2,128)S(1)}, f32[2,2,2,32,256]{4,2,3,1,0:T(2,128)}, u32[]{:S(2)}) copy-start(f32[2,2,2,32,256]{4,2,3,1,0:T(2,128)} %all-reduce.3.cloned.1.call-done) | copy-start | bytes 786436
  139.7 17.1 %all-to-all-start = ((f32[16,1,4096]{2,1,0:T(1,128)}), f32[16,1,4096]{2,1,0:T(1,128)S(1)}, u32[]{:S(2)}, u32[]{:S(2)}) async-start(f32[16,1,4096]{2,1,0:T(1,128)} %reshape.97), calls=%async_computation | async-start | bytes 524288 | tf_op jit(solution)/shard_map/all_to_all | solution.py:123
  146.5 28.5 %reduce-scatter.2.cloned.1.call-start = ((), (), s32[]{:S(2)}) async-start(), calls=%async_computation.3 | async-start | bytes 147456 | tf_op jit(solution)/shard_map/reduce_scatter | solution.py:88
Sparse Core Ops, SparseCore 0:
  105.6 20.9 all-reduce.2
  169.6 5.3 reduce-scatter.1
